TPU v7x, 32 devices: a whole 2x2x4 slice. The times are simulated.
32 devices in a mesh: gx: 4 (over z), gy: 8 (over y, x, core).
Axes of the slice: x: 2, y: 2, z: 4, core: 2. Of those that a mesh axis runs over, the one named last changes fastest.
Arguments:
- tokens: bfloat16 [512, 3584], P(('gx', 'gy')), may hold values from -6 to 6
- expert_ids: int32 [512, 8], P(('gx', 'gy')), may hold values from 0 to 31, all different within a row; in each aligned block of 16 rows (0 to 15, 16 to 31, ...) at most 6 rows name the same one
- backup_ids: int32 [512, 8], P(('gx', 'gy')), may hold values from 0 to 31, all different within a row; in each aligned block of 16 rows (0 to 15, 16 to 31, ...) at most 6 rows name the same one
- scores: float32 [512, 8], P(('gx', 'gy')), may hold values from 0.05 to 1
- gate_weight: bfloat16 [32, 3584, 1024], P(('gx', 'gy')), may hold values from -0.09375 to 0.09375
- up_weight: bfloat16 [32, 3584, 1024], P(('gx', 'gy')), may hold values from -0.09375 to 0.09375
- down_weight: bfloat16 [32, 1024, 3584], P(('gx', 'gy')), may hold values from -0.1875 to 0.1875
Outputs:
- mixed: bfloat16 [512, 3584], P(('gx', 'gy'))
Inputs may be any that keep to these rules, and one draw needn't show every extreme that they name: `expert_ids`: among the rows of one device no expert number is named more than 6 times. `backup_ids`: among the rows of one device no expert number is named more than 6 times.
All inputs are finite; a program needn't handle non-finite values.
Results may differ from a plain program's by a relative error of at most 0.0058.
Values may be sent and summed in bfloat16 or wider, within the bound.
A program may use at most 128 MiB of HBM per device.

v0:
```python
import jax
import jax.numpy as jnp
from jax import lax
from jax.sharding import PartitionSpec as P


def ranks_within(numbers, active, expert_count):
    table = (
        (numbers[:, None] == jnp.arange(expert_count, dtype=jnp.int32)[None, :]) & active[:, None]
    ).astype(jnp.int32)
    within = jnp.sum((jnp.cumsum(table, axis=0) - table) * table, axis=1)
    return (within, table)


def pack_rows(tokens, destination, active, slot_total, top_count):
    pick_number = jnp.arange(destination.shape[0], dtype=jnp.int32)
    match_grid = (
        destination[None, :] == jnp.arange(slot_total, dtype=jnp.int32)[:, None]
    ) & active[None, :]
    source = jnp.sum(jnp.where(match_grid, pick_number[None, :] + 1, 0), axis=1) - 1
    picked_rows = jnp.take(tokens, jnp.maximum(source, 0) // top_count, axis=0)
    return jnp.where((source >= 0)[:, None], picked_rows, jnp.zeros((), tokens.dtype))


def send_rows(slot_rows):
    return lax.all_to_all(slot_rows, ("gx", "gy"), split_axis=0, concat_axis=0, tiled=True)


def on_device(tokens, expert_ids, backup_ids, scores, gate_weight, up_weight, down_weight):
    device_count = lax.axis_size(("gx", "gy"))
    own_index = lax.axis_index(("gx", "gy"))
    tok_rows, top_count = expert_ids.shape
    model_width = tokens.shape[1]
    per_source = tok_rows * top_count
    spare_quota = max(1, per_source // (4 * device_count))
    most_rows = max(2, (3 * per_source + 2 * device_count - 1) // (2 * device_count))
    first_flat = expert_ids.reshape(-1)
    backup_flat = backup_ids.reshape(-1)
    everyone = jnp.ones((per_source,), dtype=bool)
    first_within, first_table = ranks_within(first_flat, everyone, device_count)
    own_counts = jnp.sum(first_table, axis=0)
    all_counts = lax.all_gather(own_counts[None, :], ("gx", "gy"), axis=0, tiled=True)
    before = jnp.cumsum(all_counts, axis=0) - all_counts
    own_before = lax.dynamic_index_in_dim(before, own_index, 0, keepdims=False)
    first_rank = jnp.sum(first_table * own_before[None, :], axis=1) + first_within
    kept_mask = first_rank < per_source
    spilled = jnp.logical_not(kept_mask)
    spill_rank = ranks_within(backup_flat, spilled, device_count)[0]
    spare_mask = spilled & (spill_rank < spare_quota)
    send_first = pack_rows(
        tokens,
        first_flat * most_rows + first_within,
        kept_mask,
        device_count * most_rows,
        top_count,
    ).reshape(device_count, most_rows, model_width)
    send_spill = pack_rows(
        tokens,
        backup_flat * spare_quota + spill_rank,
        spare_mask,
        device_count * spare_quota,
        top_count,
    ).reshape(device_count, spare_quota, model_width)
    recv_first = send_rows(send_first)
    recv_spill = send_rows(send_spill)
    count_column = lax.dynamic_index_in_dim(all_counts, own_index, 1, keepdims=False)
    before_column = lax.dynamic_index_in_dim(before, own_index, 1, keepdims=False)
    ending = before_column + count_column
    row_number = jnp.arange(per_source, dtype=jnp.int32)
    source_of_row = jnp.sum((ending[None, :] <= row_number[:, None]).astype(jnp.int32), axis=1)
    owner_grid = source_of_row[:, None] == jnp.arange(device_count, dtype=jnp.int32)[None, :]
    start_of_row = jnp.sum(jnp.where(owner_grid, before_column[None, :], 0), axis=1)
    filled = row_number < ending[device_count - 1]
    slot_index = jnp.minimum(source_of_row, device_count - 1) * most_rows + jnp.clip(
        row_number - start_of_row, 0, most_rows - 1
    )
    first_rows = jnp.take(
        recv_first.reshape(device_count * most_rows, model_width), slot_index, axis=0
    )
    first_rows = jnp.where(filled[:, None], first_rows, jnp.zeros((), first_rows.dtype))
    expert_rows = jnp.concatenate(
        [first_rows, recv_spill.reshape(device_count * spare_quota, model_width)], axis=0
    )
    gate = jnp.dot(expert_rows, gate_weight[0], preferred_element_type=jnp.float32)
    upward = jnp.dot(expert_rows, up_weight[0], preferred_element_type=jnp.float32)
    hidden = (jax.nn.silu(gate) * upward).astype(jnp.bfloat16)
    expert_out = jnp.dot(hidden, down_weight[0], preferred_element_type=jnp.float32).astype(
        jnp.bfloat16
    )
    position = jnp.arange(most_rows, dtype=jnp.int32)
    rank_grid = before_column[:, None] + position[None, :]
    live_slot = (position[None, :] < count_column[:, None]) & (rank_grid < per_source)
    back_first = jnp.take(expert_out[:per_source], jnp.clip(rank_grid, 0, per_source - 1), axis=0)
    back_first = jnp.where(live_slot[:, :, None], back_first, jnp.zeros((), back_first.dtype))
    back_spill = expert_out[per_source:].reshape(device_count, spare_quota, model_width)
    home_first = send_rows(back_first)
    home_spill = send_rows(back_spill)
    first_slot = jnp.minimum(first_flat * most_rows + first_within, device_count * most_rows - 1)
    spill_slot = backup_flat * spare_quota + jnp.minimum(spill_rank, spare_quota - 1)
    picked_first = jnp.take(
        home_first.reshape(device_count * most_rows, model_width), first_slot, axis=0
    )
    picked_spill = jnp.take(
        home_spill.reshape(device_count * spare_quota, model_width), spill_slot, axis=0
    )
    picked = jnp.where(kept_mask[:, None], picked_first, picked_spill).reshape(
        tok_rows, top_count, model_width
    )
    route_weights = scores / jnp.sum(scores, axis=1, keepdims=True)
    weights = jnp.where(
        (kept_mask | spare_mask).reshape(tok_rows, top_count),
        route_weights,
        jnp.zeros((), jnp.float32),
    )
    mixed = jnp.sum(weights[:, :, None] * picked.astype(jnp.float32), axis=1)
    return mixed.astype(jnp.bfloat16)


def solution(mesh):
    placed = (
        P(("gx", "gy"), None),
        P(("gx", "gy"), None),
        P(("gx", "gy"), None),
        P(("gx", "gy"), None),
        P(("gx", "gy"), None, None),
        P(("gx", "gy"), None, None),
        P(("gx", "gy"), None, None),
    )
    return jax.shard_map(
        on_device, mesh=mesh, in_specs=placed, out_specs=P(("gx", "gy"), None), check_vma=False
    )
```

profile of v0, /device:TPU:0, one launch (start us, length us, event | category | flops | bytes accessed | tf_op | source)
XLA Modules:
  0.0 190.5 jit_solution(3102107505313801850)
XLA Ops:
  0.0 0.8 copy.28
  0.9 0.1 fusion.24
  1.1 0.8 copy.29
  2.0 0.2 dynamic-update-slice
  2.2 0.2 copy-done.5
  2.5 42.0 %all-reduce = s32[1024]{0:T(1024)S(1)} all-reduce(s32[1024]{0:T(1024)S(1)} %dynamic-update-slice), channel_id=2, replica_groups=mesh['gx'=4,'gy'=8] {'gx','gy'}, use_global_device_ids=true, to_apply=%add | all-reduce | flops 1024 | bytes 8192
  44.6 0.2 reduce_window_sum.29
  44.8 0.2 select_reduce_fusion.3
  44.9 0.5 compare_and_fusion.1
  45.5 0.1 fusion.23
  45.6 0.2 reduce_window_sum.30
  45.7 0.2 select_reduce_fusion.2
  45.9 0.6 compare_and_fusion.3
  46.5 0.1 select_reduce_fusion.5
  46.7 0.7 gather_fusion.1
  47.4 0.1 fusion.19
  47.5 0.5 broadcast.609
  48.0 0.7 reduce.4
  48.8 0.8 reshape.518
  49.5 4.4 %all-to-all-start.1 = ((bf16[32,2,1792]{2,1,0:T(2,128)(2,1)}), bf16[32,2,1792]{2,1,0:T(2,128)(2,1)S(1)}, u32[]{:S(2)}, u32[]{:S(2)}) async-start(bf16[32,2,1792]{2,1,0:T(2,128)(2,1)} %reshape.518), calls=%async_computation.1 | async-start | bytes 458752 | tf_op jit(solution)/shard_map/all_to_all | solution.py:26
  53.9 0.1 select_reduce_fusion
  54.1 0.7 reshape.451
  54.8 0.7 div.38
  55.5 0.7 ge.61
  56.2 1.4 gather_fusion
  57.7 0.5 gather.24
  58.2 0.7 compare_and_fusion
  58.9 2.3 %select_select_fusion.1 = bf16[32,6,3584]{2,1,0:T(8,128)(2,1)} fusion(bf16[32,6,3584]{2,1,0:T(8,128)(2,1)S(1)} %gather.24, pred[32,6]{1,0:T(8,128)(4,1)S(1)} %compare_and_fusion, pred[32,6]{1,0:T(8,128)(4,1)} %ge.61), kind=kLoop, calls=%fused_computation.16 | loop fusion | flops 1376256 | bytes 2752896 | tf_op jit(solution)/shard_map/jit(_where)/select_n | solution.py:22
  61.2 2.6 %all-to-all-done.1 = bf16[32,2,1792]{2,1,0:T(2,128)(2,1)S(1)} async-done(((bf16[32,2,1792]{2,1,0:T(2,128)(2,1)}), bf16[32,2,1792]{2,1,0:T(2,128)(2,1)S(1)}, u32[]{:S(2)}, u32[]{:S(2)}) %all-to-all-start.1) | async-done | bytes 229408 | tf_op jit(solution)/shard_map/all_to_all | solution.py:26
  63.7 3.3 %all-to-all-start = ((bf16[32,6,3584]{2,1,0:T(8,128)(2,1)}), bf16[32,6,3584]{2,1,0:T(8,128)(2,1)S(1)}, u32[]{:S(2)}, u32[]{:S(2)}) async-start(bf16[32,6,3584]{2,1,0:T(8,128)(2,1)} %select_select_fusion.1), calls=%async_computation | async-start | bytes 3670016 | tf_op jit(solution)/shard_map/all_to_all | solution.py:26
  67.0 0.2 dynamic-slice_reduce_fusion
  67.2 0.6 slice.9
  67.9 0.1 reshape.489
  68.0 1.2 iota_compare_fusion.7
  69.3 0.2 select_reduce_fusion.1
  69.5 0.5 compare_and_fusion.2
  70.1 0.6 pad_clamp_fusion.4
  70.7 0.6 pad_clamp_fusion.2
  71.2 0.7 fusion.29
  71.9 0.2 reshape.519
  72.1 38.1 %all-to-all-done = bf16[32,6,3584]{2,1,0:T(8,128)(2,1)S(1)} async-done(((bf16[32,6,3584]{2,1,0:T(8,128)(2,1)}), bf16[32,6,3584]{2,1,0:T(8,128)(2,1)S(1)}, u32[]{:S(2)}, u32[]{:S(2)}) %all-to-all-start) | async-done | bytes 1376288 | tf_op jit(solution)/shard_map/all_to_all | solution.py:26
  110.2 0.5 reshape.445
  110.7 1.2 gather_fusion.4
  112.0 0.9 select_select_fusion.3
  112.8 4.4 %fusion.4 = f32[160,1024]{1,0:T(8,128)S(1)} fusion(bf16[1,3584,1024]{2,1,0:T(8,128)(2,1)} %param.13, bf16[32,3584]{1,0:T(8,128)(2,1)S(1)} %bitcast.58, bf16[128,3584]{1,0:T(8,128)(2,1)S(1)} %select_select_fusion.3), kind=kOutput, calls=%fused_computation.10 | convolution fusion | flops 1176698880 | bytes 9142272 | tf_op jit(solution)/shard_map/dot_general | solution.py:84
  117.3 7.8 %fusion.6 = bf16[160,3584]{1,0:T(8,128)(2,1)S(1)} fusion(bf16[1,1024,3584]{2,1,0:T(8,128)(2,1)} %param.15, bf16[1,3584,1024]{2,1,0:T(8,128)(2,1)} %param.14, bf16[32,3584]{1,0:T(8,128)(2,1)S(1)} %bitcast.59, bf16[128,3584]{1,0:T(8,128)(2,1)S(1)} %select_select_fusion.3, f32[160,1024]{1,0:T(8,128)S(1)} %fusion.4), kind=kOutput, calls=%fused_computation.12 | convolution fusion | flops 2352660480 | bytes 17629184 | tf_op jit(solution)/shard_map/dot_general | solution.py:87
  125.2 0.7 reduce.5
  125.9 0.8 reshape.520
  126.7 4.0 %all-to-all-start.3 = ((bf16[32,2,1792]{2,1,0:T(2,128)(2,1)}), bf16[32,2,1792]{2,1,0:T(2,128)(2,1)S(1)}, u32[]{:S(2)}, u32[]{:S(2)}) async-start(bf16[32,2,1792]{2,1,0:T(2,128)(2,1)} %reshape.520), calls=%async_computation.3 | async-start | bytes 458752 | tf_op jit(solution)/shard_map/all_to_all | solution.py:26
  130.7 1.4 gather_fusion.2
  132.2 1.5 reshape.488
  133.7 3.1 %select_select_fusion = bf16[32,6,3584]{2,1,0:T(8,128)(2,1)} fusion(bf16[32,6,3584]{2,1,0:T(8,128)(2,1)} %reshape.488, pred[32,6]{1,0:T(8,128)(4,1)S(1)} %copy-done.11, pred[32,6]{1,0:T(8,128)(4,1)S(1)} %copy-done.10), kind=kLoop, calls=%fused_computation.15 | loop fusion | flops 1376256 | bytes 2752896 | tf_op jit(solution)/shard_map/jit(_where)/select_n | solution.py:94
  136.8 3.7 %all-to-all-done.3 = bf16[32,2,1792]{2,1,0:T(2,128)(2,1)S(1)} async-done(((bf16[32,2,1792]{2,1,0:T(2,128)(2,1)}), bf16[32,2,1792]{2,1,0:T(2,128)(2,1)S(1)}, u32[]{:S(2)}, u32[]{:S(2)}) %all-to-all-start.3) | async-done | bytes 229408 | tf_op jit(solution)/shard_map/all_to_all | solution.py:26
  140.5 2.9 %all-to-all-start.2 = ((bf16[32,6,3584]{2,1,0:T(8,128)(2,1)}), bf16[32,6,3584]{2,1,0:T(8,128)(2,1)S(1)}, u32[]{:S(2)}, u32[]{:S(2)}) async-start(bf16[32,6,3584]{2,1,0:T(8,128)(2,1)} %select_select_fusion), calls=%async_computation.2 | async-start | bytes 3670016 | tf_op jit(solution)/shard_map/all_to_all | solution.py:26
  143.5 0.1 lt.166
  143.7 0.1 lt.169
  143.8 0.6 pad_clamp_fusion.1
  144.5 0.7 divide_select_fusion
  145.1 0.2 reshape.521
  145.3 2.1 %gather_fusion.3 = bf16[128,3584]{1,0:T(8,128)(2,1)} fusion(bf16[32,3584]{1,0:T(8,128)(2,1)S(1)} %bitcast.57, s32[1024]{0:T(1024)S(1)} %pad_clamp_fusion), kind=kCustom, calls=%fused_computation.5 | custom fusion | bytes 1835520 | tf_op jit(solution)/shard_map/jit(_take)/gather | solution.py:103
  147.4 39.3 %all-to-all-done.2 = bf16[32,6,3584]{2,1,0:T(8,128)(2,1)S(1)} async-done(((bf16[32,6,3584]{2,1,0:T(8,128)(2,1)}), bf16[32,6,3584]{2,1,0:T(8,128)(2,1)S(1)}, u32[]{:S(2)}, u32[]{:S(2)}) %all-to-all-start.2) | async-done | bytes 1376288 | tf_op jit(solution)/shard_map/all_to_all | solution.py:26
  186.7 0.5 reshape.447
  187.2 1.4 gather_fusion.5
  188.7 1.8 fusion.9
  (72 shorter events, 1.0 us)
Async XLA Ops:
  0.0 46.7 %copy-start = (bf16[16,3584]{1,0:T(8,128)(2,1)S(1)}, bf16[16,3584]{1,0:T(8,128)(2,1)}, u32[]{:S(2)}) copy-start(bf16[16,3584]{1,0:T(8,128)(2,1)} %param.9) | copy-start | bytes 344068
  1.9 0.6 copy-start.5
  44.5 2.2 %copy-start.2 = (s32[32,32]{1,0:T(8,128)}, s32[32,32]{1,0:T(8,128)S(1)}, u32[]{:S(2)}) copy-start(s32[32,32]{1,0:T(8,128)S(1)} %reshape.503) | copy-start | bytes 12292
  44.6 2.1 %copy-start.7 = (s32[32,32]{1,0:T(8,128)}, s32[32,32]{1,0:T(8,128)S(1)}, u32[]{:S(2)}) copy-start(s32[32,32]{1,0:T(8,128)S(1)} %sub.36) | copy-start | bytes 12292
  45.5 8.4 %copy-start.13 = (pred[128]{0:T(512)(128)(4,1)}, pred[128]{0:T(512)(128)(4,1)S(1)}, u32[]{:S(2)}) copy-start(pred[128]{0:T(512)(128)(4,1)S(1)} %get-tuple-element.23) | copy-start | bytes 388
  45.9 0.8 copy-start.16
  49.5 14.2 %all-to-all-start.1 = ((bf16[32,2,1792]{2,1,0:T(2,128)(2,1)}), bf16[32,2,1792]{2,1,0:T(2,128)(2,1)S(1)}, u32[]{:S(2)}, u32[]{:S(2)}) async-start(bf16[32,2,1792]{2,1,0:T(2,128)(2,1)} %reshape.518), calls=%async_computation.1 | async-start | bytes 458752 | tf_op jit(solution)/shard_map/all_to_all | solution.py:26
  61.2 5.8 %copy-start.3 = (s32[32,32]{1,0:T(8,128)S(1)}, s32[32,32]{1,0:T(8,128)}, u32[]{:S(2)}) copy-start(s32[32,32]{1,0:T(8,128)} %copy-done.2) | copy-start | bytes 12292
  61.2 5.9 %copy-start.8 = (s32[32,32]{1,0:T(8,128)S(1)}, s32[32,32]{1,0:T(8,128)}, u32[]{:S(2)}) copy-start(s32[32,32]{1,0:T(8,128)} %copy-done.7) | copy-start | bytes 12292
  63.7 46.5 %all-to-all-start = ((bf16[32,6,3584]{2,1,0:T(8,128)(2,1)}), bf16[32,6,3584]{2,1,0:T(8,128)(2,1)S(1)}, u32[]{:S(2)}, u32[]{:S(2)}) async-start(bf16[32,6,3584]{2,1,0:T(8,128)(2,1)} %select_select_fusion.1), calls=%async_computation | async-start | bytes 3670016 | tf_op jit(solution)/shard_map/all_to_all | solution.py:26
  125.1 5.6 %copy-start.4 = (s32[1024]{0:T(1024)S(1)}, s32[1024]{0:T(1024)}, u32[]{:S(2)}) copy-start(s32[1024]{0:T(1024)} %pad_clamp_fusion.2) | copy-start | bytes 12292
  126.7 13.8 %all-to-all-start.3 = ((bf16[32,2,1792]{2,1,0:T(2,128)(2,1)}), bf16[32,2,1792]{2,1,0:T(2,128)(2,1)S(1)}, u32[]{:S(2)}, u32[]{:S(2)}) async-start(bf16[32,2,1792]{2,1,0:T(2,128)(2,1)} %reshape.520), calls=%async_computation.3 | async-start | bytes 458752 | tf_op jit(solution)/shard_map/all_to_all | solution.py:26
  132.2 1.5 copy-start.10
  132.2 1.5 copy-start.11
  136.8 6.6 %copy-start.6 = (s32[16,8]{1,0:T(8,128)S(1)}, s32[16,8]{1,0:T(8,128)}, u32[]{:S(2)}) copy-start(s32[16,8]{1,0:T(8,128)} %copy-done.5) | copy-start | bytes 1540
  136.8 6.7 %copy-start.14 = (pred[128]{0:T(512)(128)(4,1)S(1)}, pred[128]{0:T(512)(128)(4,1)}, u32[]{:S(2)}) copy-start(pred[128]{0:T(512)(128)(4,1)} %copy-done.13) | copy-start | bytes 388
  136.8 6.8 %copy-start.12 = (f32[16,8]{0,1:T(8,128)S(1)}, f32[16,8]{0,1:T(8,128)}, u32[]{:S(2)}) copy-start(f32[16,8]{0,1:T(8,128)} %param.12) | copy-start | bytes 1540
  136.8 6.9 %copy-start.18 = (pred[128]{0:T(512)(128)(4,1)S(1)}, pred[128]{0:T(512)(128)(4,1)}, u32[]{:S(2)}) copy-start(pred[128]{0:T(512)(128)(4,1)} %get-tuple-element.19) | copy-start | bytes 388
  136.8 7.0 %copy-start.19 = (s32[128]{0:T(128)S(1)}, s32[128]{0:T(128)}, u32[]{:S(2)}) copy-start(s32[128]{0:T(128)} %get-tuple-element.9) | copy-start | bytes 1540
  136.8 7.6 %copy-start.17 = (s32[128]{0:T(128)S(1)}, s32[128]{0:T(128)}, u32[]{:S(2)}) copy-start(s32[128]{0:T(128)} %copy-done.16) | copy-start | bytes 1540
  140.5 46.2 %all-to-all-start.2 = ((bf16[32,6,3584]{2,1,0:T(8,128)(2,1)}), bf16[32,6,3584]{2,1,0:T(8,128)(2,1)S(1)}, u32[]{:S(2)}, u32[]{:S(2)}) async-start(bf16[32,6,3584]{2,1,0:T(8,128)(2,1)} %select_select_fusion), calls=%async_computation.2 | async-start | bytes 3670016 | tf_op jit(solution)/shard_map/all_to_all | solution.py:26
  187.2 1.4 copy-start.1
  187.2 1.4 copy-start.9
  187.2 1.4 copy-start.15
  187.2 1.4 copy-start.20
  187.2 1.4 copy-start.21
where the time goes:
time: 191 us; the launch traced here: 190 us
  waiting for transfers between devices  83.7 us (44%)
  blocking collectives  42 us (22%)
  local copies, waits for them, and re-layouts  19.4 us (10%)
  other arithmetic  18.1 us (9%)
  starting transfers between devices  14.6 us (8%)
  matrix products  12.3 us (6%)
    all_to_all x4, waiting for transfers between devices, send_rows(): lax.all_to_all(slot_rows, ('gx', 'gy'), split_axis=0, concat_axis=0, tile...  83.7 us
    unnamed x1, blocking collectives  42 us
    all_to_all x4, starting transfers between devices, send_rows(): lax.all_to_all(slot_rows, ('gx', 'gy'), split_axis=0, concat_axis=0, tile...  14.6 us
    dot_general x1, matrix products, on_device(): jnp.dot(hidden, down_weight[0], preferred_element_type=jnp.float32)  7.82 us
    dot_general x1, matrix products, on_device(): jnp.dot(expert_rows, gate_weight[0], preferred_element_type=jnp.float32)  4.44 us
    unnamed x55, local copies, waits for them, and re-layouts  4.11 us
  transfers between devices with their start and end apart: 4, of which 4 were waited for; matrix products, arithmetic and copies ran while one was open for 12% of the time, Pallas kernels for 0%

commit v1 on v0

--- a/solution.py
+++ b/solution.py
@@ -1,6 +1,9 @@
+import functools
 import jax
 import jax.numpy as jnp
 from jax import lax
+from jax.experimental import pallas as pl
+from jax.experimental.pallas import tpu as pltpu
 from jax.sharding import PartitionSpec as P
 
 
@@ -116,6 +119,277 @@
     return mixed.astype(jnp.bfloat16)
 
 
+def exchange(cfg, tok_ref, meta_ref, gate_hbm, up_hbm, down_hbm, out_ref,
+             metas, toks, wg, wu, wd, pick, comb_hi, comb_lo, gate, upward, hidden,
+             own, to_core, from_core, to_one, from_one, to_two, from_two, to_z, from_z,
+             ag_send, ag_recv, rs_send, rs_recv, w_sem):
+    parts, width, cap, quota, slots, top = cfg
+    z = lax.axis_index("gx")
+    g = lax.axis_index("gy")
+    c = lax.rem(g, 2)
+    x = lax.rem(lax.div(g, 2), 2)
+    y = lax.div(g, 4)
+    core_peer = (z, g + 1 - 2 * c)
+    x_peer = (z, g + 2 - 4 * x)
+    y_peer = (z, g + 4 - 8 * y)
+    z_peers = [(lax.rem(z + hop, 4), g) for hop in (1, 2, 3)]
+    expert = z * 8 + g
+
+    def remote(src, dst, sems, device):
+        return pltpu.make_async_remote_copy(
+            src_ref=src, dst_ref=dst, send_sem=sems[0], recv_sem=sems[1],
+            device_id=device, device_id_type=pl.DeviceIdType.MESH)
+
+    weight_copies = []
+    for j in range(parts):
+        rows = pl.ds(j * width, width)
+        pair = [pltpu.make_async_copy(gate_hbm.at[0, rows], wg.at[rows], w_sem.at[0, j]),
+                pltpu.make_async_copy(up_hbm.at[0, rows], wu.at[rows], w_sem.at[1, j])]
+        weight_copies.append(pair)
+        for copy in pair:
+            copy.start()
+    down_copies = []
+    for j in range(parts):
+        copy = pltpu.make_async_copy(down_hbm.at[0, :, pl.ds(j * width, width)], wd.at[j], w_sem.at[2, j])
+        copy.start()
+        down_copies.append(copy)
+
+    barrier = pltpu.get_barrier_semaphore()
+    for peer in [core_peer, x_peer, y_peer] + z_peers:
+        pl.semaphore_signal(barrier, inc=1, device_id=peer, device_id_type=pl.DeviceIdType.MESH)
+    metas[z, y, x, c] = meta_ref[...]
+    for j in range(parts):
+        toks[j, z, y, x, c] = tok_ref[:, j * width:(j + 1) * width]
+    pl.semaphore_wait(barrier, 6)
+
+    items = [metas] + [toks.at[j] for j in range(parts)]
+    started = []
+
+    def gather_copies(i):
+        buf = items[i]
+        sem = lambda k: (ag_send.at[i, k], ag_recv.at[i, k])
+        mine = buf.at[z, y, x, c]
+        copies = [[remote(mine, mine, sem(k), z_peers[k]) for k in range(3)]]
+        line = buf.at[:, y, x, c]
+        if i % 2 == 0:
+            plane = buf.at[:, y, :, c]
+            copies += [[remote(line, line, sem(3), x_peer)], [remote(plane, plane, sem(4), y_peer)]]
+        else:
+            plane = buf.at[:, :, x, c]
+            copies += [[remote(line, line, sem(3), y_peer)], [remote(plane, plane, sem(4), x_peer)]]
+        whole = buf.at[:, :, :, c]
+        copies += [[remote(whole, whole, sem(5), core_peer)]]
+        return copies
+
+    gathers = [gather_copies(i) for i in range(len(items))]
+
+    def begin(group):
+        for copy in group:
+            copy.start()
+            started.append(copy)
+
+    def arrive(group):
+        for copy in group:
+            copy.wait_recv()
+
+    def route():
+        record = metas[...].reshape(512, 128)
+        first, backup, weight = record[:, 0:top], record[:, top:2 * top], record[:, 2 * top:3 * top]
+        lane = lax.broadcasted_iota(jnp.int32, (512, 128), 1).astype(jnp.float32)
+        named = jnp.zeros((512, 128), jnp.float32)
+        for k in range(top):
+            named += jnp.where(first[:, k:k + 1] == lane, 1.0, 0.0)
+        row = lax.broadcasted_iota(jnp.int32, (512, 512), 0)
+        col = lax.broadcasted_iota(jnp.int32, (512, 512), 1)
+        lower = jnp.where(col < row, 1.0, 0.0)
+        rank = jnp.dot(lower.astype(jnp.bfloat16), named.astype(jnp.bfloat16), preferred_element_type=jnp.float32)
+        spilled = jnp.where(rank >= cap, named, 0.0)
+        me = expert.astype(jnp.float32)
+        is_me = jnp.where(lane == me, 1.0, 0.0)
+        my_named = jnp.sum(is_me * named, axis=1, keepdims=True)
+        my_rank = jnp.sum(is_me * rank, axis=1, keepdims=True)
+        my_weight = jnp.sum(jnp.where(first == me, weight, 0.0), axis=1, keepdims=True)
+        has_backup = jnp.sum(jnp.where(backup == me, 1.0, 0.0), axis=1, keepdims=True)
+        its_first = jnp.sum(jnp.where(backup == me, first, 0.0), axis=1, keepdims=True)
+        its_weight = jnp.sum(jnp.where(backup == me, weight, 0.0), axis=1, keepdims=True)
+        moved = has_backup * jnp.sum(jnp.where(lane == its_first, spilled, 0.0), axis=1, keepdims=True)
+        near = jnp.where(lax.div(row, 16) == lax.div(col, 16), lower, 0.0)
+        moved_wide = jnp.broadcast_to(moved, (512, 128))
+        spill_rank = jnp.dot(near.astype(jnp.bfloat16), moved_wide.astype(jnp.bfloat16),
+                             preferred_element_type=jnp.float32)
+        block = lax.div(lax.broadcasted_iota(jnp.int32, (512, 128), 0), 16).astype(jnp.float32)
+        kept_grid = jnp.where(my_rank == lane, my_named, 0.0)
+        spare_grid = jnp.where(spill_rank < quota, jnp.where(block * quota + spill_rank == lane, moved_wide, 0.0), 0.0)
+        grid = jnp.concatenate([kept_grid, spare_grid], axis=1)
+        pick[...] = grid.T[:slots].astype(jnp.bfloat16)
+        mixing = jnp.concatenate([kept_grid * my_weight, spare_grid * its_weight], axis=1)[:, :slots]
+        high = mixing.astype(jnp.bfloat16)
+        comb_hi[...] = high.reshape(16, 2, 16, slots)
+        comb_lo[...] = (mixing - high.astype(jnp.float32)).astype(jnp.bfloat16).reshape(16, 2, 16, slots)
+
+    def project(j):
+        for copy in weight_copies[j]:
+            copy.wait()
+        rows = jnp.dot(pick[...], toks[j].reshape(512, width), preferred_element_type=jnp.float32).astype(jnp.bfloat16)
+        part = pl.ds(j * width, width)
+        new_gate = jnp.dot(rows, wg[part, :], preferred_element_type=jnp.float32)
+        new_up = jnp.dot(rows, wu[part, :], preferred_element_type=jnp.float32)
+        if j == 0:
+            gate[...] = new_gate
+            upward[...] = new_up
+        elif j < parts - 1:
+            gate[...] += new_gate
+            upward[...] += new_up
+        else:
+            full = gate[...] + new_gate
+            hidden[...] = (full / (1.0 + jnp.exp(-full)) * (upward[...] + new_up)).astype(jnp.bfloat16)
+
+    count = len(items)
+    for step in range(count + 4):
+        if step < count:
+            begin(gathers[step][0])
+        for stage in (1, 2, 3):
+            i = step - stage
+            if 0 <= i < count:
+                arrive(gathers[i][stage - 1])
+                begin(gathers[i][stage])
+        i = step - 4
+        if 0 <= i < count:
+            arrive(gathers[i][3])
+            if i == 0:
+                route()
+            else:
+                project(i - 1)
+
+    def scatter_copies(j):
+        sem = lambda k: (rs_send.at[j, k], rs_recv.at[j, k])
+        one, two = (y_peer, x_peer) if j % 2 == 0 else (x_peer, y_peer)
+        return [[remote(to_core.at[j], from_core.at[j], sem(0), core_peer)],
+                [remote(to_one.at[j], from_one.at[j], sem(1), one)],
+                [remote(to_two.at[j], from_two.at[j], sem(2), two)],
+                [remote(to_z.at[j, k], from_z.at[j, k], sem(3 + k), z_peers[k]) for k in range(3)]]
+
+    scatters = [scatter_copies(j) for j in range(parts)]
+    f32 = jnp.float32
+
+    def produce(j):
+        down_copies[j].wait()
+        rows = jnp.dot(hidden[...], wd[j], preferred_element_type=f32).astype(jnp.bfloat16)
+
+        def combine(core):
+            high = comb_hi[:, core].reshape(256, slots)
+            low = comb_lo[:, core].reshape(256, slots)
+            return (jnp.dot(high, rows, preferred_element_type=f32) + jnp.dot(low, rows, preferred_element_type=f32))
+
+        to_core[j] = combine(1 - c).astype(jnp.bfloat16).reshape(4, 2, 2, 16, width)
+        begin(scatters[j][0])
+        own[j] = combine(c).reshape(4, 2, 2, 16, width)
+
+    def at_one(j, zz, first, second):
+        yy, xx = (first, second) if j % 2 == 0 else (second, first)
+        return own[j, zz, yy, xx] + from_core[j, zz, yy, xx].astype(f32)
+
+    def after_core(j):
+        first = y if j % 2 == 0 else x
+
+        @pl.loop(0, 4)
+        def _(zz):
+            for second in range(2):
+                to_one[j, zz, second] = at_one(j, zz, 1 - first, second).astype(jnp.bfloat16)
+
+        begin(scatters[j][1])
+
+    def at_two(j, zz, first, second):
+        return at_one(j, zz, first, second) + from_one[j, zz, second].astype(f32)
+
+    def after_one(j):
+        first, second = (y, x) if j % 2 == 0 else (x, y)
+
+        @pl.loop(0, 4)
+        def _(zz):
+            to_two[j, zz] = at_two(j, zz, first, 1 - second).astype(jnp.bfloat16)
+
+        begin(scatters[j][2])
+
+    def at_z(j, zz):
+        first, second = (y, x) if j % 2 == 0 else (x, y)
+        return at_two(j, zz, first, second) + from_two[j, zz].astype(f32)
+
+    def after_two(j):
+        for k in range(3):
+            to_z[j, k] = at_z(j, z_peers[k][0]).astype(jnp.bfloat16)
+        begin(scatters[j][3])
+
+    def finish(j):
+        total = at_z(j, z)
+        for k in range(3):
+            total += from_z[j, k].astype(f32)
+        out_ref[:, j * width:(j + 1) * width] = total.astype(jnp.bfloat16)
+
+    steps = (after_core, after_one, after_two, finish)
+    for step in range(parts + 4):
+        if step < parts:
+            produce(step)
+        for stage in range(4):
+            j = step - 1 - stage
+            if 0 <= j < parts:
+                arrive(scatters[j][stage])
+                steps[stage](j)
+
+    for copy in started:
+        copy.wait_send()
+
+
+def fused_body(parts, tokens, expert_ids, backup_ids, scores, gate_weight, up_weight, down_weight):
+    device_count = lax.axis_size(("gx", "gy"))
+    tok_rows, top = expert_ids.shape
+    model, ff = gate_weight.shape[1:]
+    cap = tok_rows * top
+    quota = max(1, cap // (4 * device_count))
+    slots = cap + device_count * quota
+    width = model // parts
+    route_weights = scores / jnp.sum(scores, axis=1, keepdims=True)
+    meta = jnp.concatenate(
+        [expert_ids.astype(jnp.float32), backup_ids.astype(jnp.float32), route_weights,
+         jnp.zeros((tok_rows, 128 - 3 * top), jnp.float32)], axis=1)
+    bf16, f32 = jnp.bfloat16, jnp.float32
+    grid = (4, 2, 2)
+    vmem = lambda shape, kind: pltpu.VMEM(shape, kind)
+    scratch = [
+        vmem(grid + (2, tok_rows, 128), f32),
+        vmem((parts,) + grid + (2, tok_rows, width), bf16),
+        vmem((model, ff), bf16), vmem((model, ff), bf16), vmem((parts, ff, width), bf16),
+        vmem((slots, 512), bf16),
+        vmem((16, 2, tok_rows, slots), bf16), vmem((16, 2, tok_rows, slots), bf16),
+        vmem((slots, ff), f32), vmem((slots, ff), f32), vmem((slots, ff), bf16),
+        vmem((parts,) + grid + (tok_rows, width), f32),
+        vmem((parts,) + grid + (tok_rows, width), bf16), vmem((parts,) + grid + (tok_rows, width), bf16),
+        vmem((parts, 4, 2, tok_rows, width), bf16), vmem((parts, 4, 2, tok_rows, width), bf16),
+        vmem((parts, 4, tok_rows, width), bf16), vmem((parts, 4, tok_rows, width), bf16),
+        vmem((parts, 3, tok_rows, width), bf16), vmem((parts, 3, tok_rows, width), bf16),
+        pltpu.SemaphoreType.DMA((parts + 1, 6)), pltpu.SemaphoreType.DMA((parts + 1, 6)),
+        pltpu.SemaphoreType.DMA((parts, 6)), pltpu.SemaphoreType.DMA((parts, 6)),
+        pltpu.SemaphoreType.DMA((3, parts)),
+    ]
+    whole = pl.BlockSpec(memory_space=pltpu.VMEM)
+    away = pl.BlockSpec(memory_space=pl.ANY)
+    return pl.pallas_call(
+        functools.partial(exchange, (parts, width, cap, quota, slots, top)),
+        out_shape=jax.ShapeDtypeStruct((tok_rows, model), bf16),
+        in_specs=[whole, whole, away, away, away],
+        out_specs=whole,
+        scratch_shapes=scratch,
+        compiler_params=pltpu.CompilerParams(
+            collective_id=0, has_side_effects=True, vmem_limit_bytes=60 * 1024 * 1024),
+    )(tokens, meta, gate_weight, up_weight, down_weight)
+
+
+def pick_body(mesh):
+    if mesh.shape["gx"] == 4 and mesh.shape["gy"] == 8:
+        return functools.partial(fused_body, 4)
+    return on_device
+
+
 def solution(mesh):
     placed = (
         P(("gx", "gy"), None),
@@ -127,5 +401,5 @@
         P(("gx", "gy"), None, None),
     )
     return jax.shard_map(
-        on_device, mesh=mesh, in_specs=placed, out_specs=P(("gx", "gy"), None), check_vma=False
-    )
+        pick_body(mesh), mesh=mesh, in_specs=placed, out_specs=P(("gx", "gy"), None), check_vma=False
+    )

time: 191 us -> 71.5 us (0.37)
  waiting for transfers between devices: 83.7 us -> 0 us
  Pallas kernels: 0 us -> 65.8 us
  blocking collectives: 42 us -> 0 us
  local copies, waits for them, and re-layouts: 19.4 us -> 2.54 us
  other arithmetic: 18.1 us -> 2.84 us
  starting transfers between devices: 14.6 us -> 0 us
  matrix products: 12.3 us -> 0 us
    all_to_all x4 -> x0, waiting for transfers between devices: 83.7 us -> none  [send_rows(): lax.all_to_all(slot_rows, ('gx', 'gy'), split_axis=0, concat_axis=0, tile...]
    pallas_call x0 -> x1, Pallas kernels: none -> 65.8 us  [fused_body(): pl.pallas_call(functools.partial(exchange, (parts, width, cap, quota, slo...]
    unnamed x1 -> x0, blocking collectives: 42 us -> none
    all_to_all x4 -> x0, starting transfers between devices: 14.6 us -> none  [send_rows(): lax.all_to_all(slot_rows, ('gx', 'gy'), split_axis=0, concat_axis=0, tile...]
    dot_general x2 -> x0, matrix products: 12.3 us -> none  [the longest x1 7.82 us: on_device(): jnp.dot(hidden, down_weight[0], preferred_element_type=jnp.float32)]
    gather x8 -> x0, local copies, waits for them, and re-layouts: 10.2 us -> none  [the longest x2 2.93 us: on_device(): jnp.take(expert_out[:per_source], jnp.clip(rank_grid, 0, per_source - 1),...]
    select_n x10 -> x0, other arithmetic: 7.84 us -> none  [the longest x1 3.1 us: on_device(): jnp.where(live_slot[:, :, None], back_first, jnp.zeros((), back_first.dty...]
    and x5 -> x0, other arithmetic: 3.05 us -> none  [the longest x1 0.73 us: pack_rows(): picked_rows = jnp.take(tokens, jnp.maximum(source, 0) // top_count, axis=0)]
  transfers between devices with their start and end apart: 4 -> 0, of which waited for: 4 -> 0; matrix products, arithmetic and copies ran while one was open for 12% -> 0% of each run, Pallas kernels for 0% -> 0%
where the time goes in v1:
time: 71.5 us; the launch traced here: 71.2 us
  Pallas kernels  65.8 us (92%)
  other arithmetic  2.84 us (4%)
  local copies, waits for them, and re-layouts  2.54 us (4%)
    pallas_call x1, Pallas kernels, fused_body(): pl.pallas_call(functools.partial(exchange, (parts, width, cap, quota, slo...  65.8 us
    unnamed x2, local copies, waits for them, and re-layouts  2.31 us

profile of v1, /device:TPU:0, one launch (start us, length us, event | category | flops | bytes accessed | tf_op | source)
XLA Modules:
  0.0 71.2 jit_solution(7859036572782729424)
XLA Ops:
  0.0 0.7 reduce_sum.9
  0.7 0.1 pad.3.clone
  0.8 0.7 convert_element_type.6
  1.5 0.1 copy.13
  1.5 0.7 convert_element_type.7
  2.2 0.1 copy.14
  2.3 0.8 %copy.11 = f32[16,8]{1,0:T(8,128)S(1)} copy(f32[16,8]{0,1:T(8,128)} %param.10) | data formatting | bytes 1024 | tf_op args[3]
  3.1 0.1 broadcast_divide_fusion
  3.1 0.7 maximum_maximum_fusion.meta_ref
  3.8 65.8 %shard_map.73 = bf16[16,3584]{1,0:T(8,128)(2,1)} custom-call(bf16[16,3584]{1,0:T(8,128)(2,1)} %tok_ref.1, f32[16,128]{1,0:T(8,128)} %maximum_maximum_fusion.meta_ref, bf16[1,3584,1024]{2,1,0:T(8,128)(2,1)} %gate_hbm.1, bf16[1,3584,1024]{2,1,0:T(8,128)(2,1)} %up_hbm.1, bf16[1,1024,3584]{2,1,0:T(8,128)(2,1)} %down_hbm.1), custom_call_target="tpu_custom_call" | custom-call | tf_op jit(solution)/shard_map/pallas_call | solution.py:376
  69.6 1.6 %copy.16 = bf16[16,3584]{1,0:T(8,128)(2,1)} copy(bf16[16,3584]{1,0:T(8,128)(2,1)} %shard_map.73) | data formatting | bytes 229376
  (1 shorter events, 0.0 us)

commit v2 on v1

--- a/solution.py
+++ b/solution.py
@@ -119,10 +119,10 @@
     return mixed.astype(jnp.bfloat16)
 
 
-def exchange(cfg, tok_ref, meta_ref, gate_hbm, up_hbm, down_hbm, out_ref,
-             metas, toks, wg, wu, wd, pick, comb_hi, comb_lo, gate, upward, hidden,
+def exchange(cfg, tok_ref, ids_ref, backups_ref, scores_ref, gate_hbm, up_hbm, down_hbm, out_ref,
+             flipped, metas, toks, wg, wu, wd, pick, comb_hi, comb_lo, gate, upward, hidden,
              own, to_core, from_core, to_one, from_one, to_two, from_two, to_z, from_z,
-             ag_send, ag_recv, rs_send, rs_recv, w_sem):
+             meta_send, meta_recv, ag_send, ag_recv, rs_send, rs_recv, w_sem):
     parts, width, cap, quota, slots, top = cfg
     z = lax.axis_index("gx")
     g = lax.axis_index("gy")
@@ -132,7 +132,8 @@
     core_peer = (z, g + 1 - 2 * c)
     x_peer = (z, g + 2 - 4 * x)
     y_peer = (z, g + 4 - 8 * y)
-    z_peers = [(lax.rem(z + hop, 4), g) for hop in (1, 2, 3)]
+    z_near = [z + 1 - 2 * lax.rem(z, 2), z + 2 - 4 * lax.div(z, 2), 3 - z]
+    z_peers = [(there, g) for there in z_near]
     expert = z * 8 + g
 
     def remote(src, dst, sems, device):
@@ -157,31 +158,16 @@
     barrier = pltpu.get_barrier_semaphore()
     for peer in [core_peer, x_peer, y_peer] + z_peers:
         pl.semaphore_signal(barrier, inc=1, device_id=peer, device_id_type=pl.DeviceIdType.MESH)
-    metas[z, y, x, c] = meta_ref[...]
+    scores = scores_ref[...]
+    flipped[0:3 * top, 0:16] = jnp.concatenate(
+        [ids_ref[...].astype(jnp.float32), backups_ref[...].astype(jnp.float32),
+         scores / jnp.sum(scores, axis=0, keepdims=True)], axis=0)
+    metas[z, y, x, c] = flipped[...].T[0:16]
     for j in range(parts):
         toks[j, z, y, x, c] = tok_ref[:, j * width:(j + 1) * width]
     pl.semaphore_wait(barrier, 6)
 
-    items = [metas] + [toks.at[j] for j in range(parts)]
     started = []
-
-    def gather_copies(i):
-        buf = items[i]
-        sem = lambda k: (ag_send.at[i, k], ag_recv.at[i, k])
-        mine = buf.at[z, y, x, c]
-        copies = [[remote(mine, mine, sem(k), z_peers[k]) for k in range(3)]]
-        line = buf.at[:, y, x, c]
-        if i % 2 == 0:
-            plane = buf.at[:, y, :, c]
-            copies += [[remote(line, line, sem(3), x_peer)], [remote(plane, plane, sem(4), y_peer)]]
-        else:
-            plane = buf.at[:, :, x, c]
-            copies += [[remote(line, line, sem(3), y_peer)], [remote(plane, plane, sem(4), x_peer)]]
-        whole = buf.at[:, :, :, c]
-        copies += [[remote(whole, whole, sem(5), core_peer)]]
-        return copies
-
-    gathers = [gather_copies(i) for i in range(len(items))]
 
     def begin(group):
         for copy in group:
@@ -191,6 +177,31 @@
     def arrive(group):
         for copy in group:
             copy.wait_recv()
+
+    def unit_copies(buf, send, recv, at, zz, flip):
+        line, whole = buf.at[zz, y, x, c], buf.at[zz, :, :, c]
+        plane = buf.at[zz, :, x, c] if flip else buf.at[zz, y, :, c]
+        one, two = (y_peer, x_peer) if flip else (x_peer, y_peer)
+        return [[remote(line, line, (send.at[at], recv.at[at]), one)],
+                [remote(plane, plane, (send.at[at + 1], recv.at[at + 1]), two)],
+                [remote(whole, whole, (send.at[at + 2], recv.at[at + 2]), core_peer)]]
+
+    mine = metas.at[z, y, x, c]
+    meta_z = [remote(mine, mine, (meta_send.at[k], meta_recv.at[k]), z_peers[k]) for k in range(3)]
+    line, plane, whole = metas.at[:, y, x, c], metas.at[:, y, :, c], metas.at[:, :, :, c]
+    meta_rest = [remote(part, part, (meta_send.at[3 + k], meta_recv.at[3 + k]), peer)
+                 for k, (part, peer) in enumerate(((line, x_peer), (plane, y_peer), (whole, core_peer)))]
+    token_z = []
+    for j in range(parts):
+        mine = toks.at[j, z, y, x, c]
+        token_z.append([remote(mine, mine, (ag_send.at[j, k], ag_recv.at[j, k]), z_peers[k]) for k in range(3)])
+    z_order = [z] + z_near
+    units = [(p, b) for p in range(parts // 2) for b in range(4)]
+    gathers = []
+    for p, b in units:
+        pair = [unit_copies(toks.at[j], ag_send.at[j], ag_recv.at[j], 3 + 3 * b, z_order[b], j % 2 == 1)
+                for j in (2 * p, 2 * p + 1)]
+        gathers.append([pair[0][stage] + pair[1][stage] for stage in range(3)])
 
     def route():
         record = metas[...].reshape(512, 128)
@@ -244,32 +255,54 @@
             full = gate[...] + new_gate
             hidden[...] = (full / (1.0 + jnp.exp(-full)) * (upward[...] + new_up)).astype(jnp.bfloat16)
 
-    count = len(items)
-    for step in range(count + 4):
-        if step < count:
+    begin(meta_z)
+    begin(gathers[0][0])
+    for p in range(parts // 2):
+        for k in range(3):
+            begin([token_z[2 * p][k], token_z[2 * p + 1][k]])
+    count = len(units)
+    for step in range(count + 3):
+        if step == 1:
+            arrive(meta_z)
+            begin(meta_rest[0:1])
+        if 2 <= step <= 3:
+            arrive(meta_rest[step - 2:step - 1])
+            begin(meta_rest[step - 1:step])
+        if 0 < step < count:
+            p, b = units[step]
+            if b > 0:
+                arrive([token_z[2 * p][b - 1], token_z[2 * p + 1][b - 1]])
             begin(gathers[step][0])
-        for stage in (1, 2, 3):
+        for stage in (1, 2):
             i = step - stage
             if 0 <= i < count:
                 arrive(gathers[i][stage - 1])
                 begin(gathers[i][stage])
-        i = step - 4
+        if step == 4:
+            arrive(meta_rest[2:3])
+            route()
+        i = step - 3
         if 0 <= i < count:
-            arrive(gathers[i][3])
-            if i == 0:
-                route()
-            else:
-                project(i - 1)
-
-    def scatter_copies(j):
+            arrive(gathers[i][2])
+            if units[i][1] == 3:
+                project(2 * units[i][0])
+                project(2 * units[i][0] + 1)
+
+    core_copies = [remote(to_core.at[j], from_core.at[j], (rs_send.at[j, 0], rs_recv.at[j, 0]), core_peer)
+                   for j in range(parts)]
+    back_order = [z_near[2], z_near[1], z_near[0], z]
+
+    def scatter_copies(j, b):
+        zz = back_order[b]
+        one, two = (y_peer, x_peer) if j % 2 == 0 else (x_peer, y_peer)
         sem = lambda k: (rs_send.at[j, k], rs_recv.at[j, k])
-        one, two = (y_peer, x_peer) if j % 2 == 0 else (x_peer, y_peer)
-        return [[remote(to_core.at[j], from_core.at[j], sem(0), core_peer)],
-                [remote(to_one.at[j], from_one.at[j], sem(1), one)],
-                [remote(to_two.at[j], from_two.at[j], sem(2), two)],
-                [remote(to_z.at[j, k], from_z.at[j, k], sem(3 + k), z_peers[k]) for k in range(3)]]
-
-    scatters = [scatter_copies(j) for j in range(parts)]
+        copies = [remote(to_one.at[j, zz], from_one.at[j, zz], sem(1 + 3 * b), one),
+                  remote(to_two.at[j, zz], from_two.at[j, zz], sem(2 + 3 * b), two)]
+        if b < 3:
+            copies.append(remote(to_z.at[j, b], from_z.at[j, b], sem(3 + 3 * b), z_peers[2 - b]))
+        return copies
+
+    scatters = [[scatter_copies(j, b) for j in (2 * p, 2 * p + 1)] for p, b in units]
     f32 = jnp.float32
 
     def produce(j):
@@ -282,43 +315,28 @@
             return (jnp.dot(high, rows, preferred_element_type=f32) + jnp.dot(low, rows, preferred_element_type=f32))
 
         to_core[j] = combine(1 - c).astype(jnp.bfloat16).reshape(4, 2, 2, 16, width)
-        begin(scatters[j][0])
+        begin([core_copies[j]])
         own[j] = combine(c).reshape(4, 2, 2, 16, width)
 
     def at_one(j, zz, first, second):
         yy, xx = (first, second) if j % 2 == 0 else (second, first)
         return own[j, zz, yy, xx] + from_core[j, zz, yy, xx].astype(f32)
 
-    def after_core(j):
+    def after_core(j, zz):
         first = y if j % 2 == 0 else x
-
-        @pl.loop(0, 4)
-        def _(zz):
-            for second in range(2):
-                to_one[j, zz, second] = at_one(j, zz, 1 - first, second).astype(jnp.bfloat16)
-
-        begin(scatters[j][1])
+        for second in range(2):
+            to_one[j, zz, second] = at_one(j, zz, 1 - first, second).astype(jnp.bfloat16)
 
     def at_two(j, zz, first, second):
         return at_one(j, zz, first, second) + from_one[j, zz, second].astype(f32)
 
-    def after_one(j):
+    def after_one(j, zz):
         first, second = (y, x) if j % 2 == 0 else (x, y)
-
-        @pl.loop(0, 4)
-        def _(zz):
-            to_two[j, zz] = at_two(j, zz, first, 1 - second).astype(jnp.bfloat16)
-
-        begin(scatters[j][2])
+        to_two[j, zz] = at_two(j, zz, first, 1 - second).astype(jnp.bfloat16)
 
     def at_z(j, zz):
         first, second = (y, x) if j % 2 == 0 else (x, y)
         return at_two(j, zz, first, second) + from_two[j, zz].astype(f32)
-
-    def after_two(j):
-        for k in range(3):
-            to_z[j, k] = at_z(j, z_peers[k][0]).astype(jnp.bfloat16)
-        begin(scatters[j][3])
 
     def finish(j):
         total = at_z(j, z)
@@ -326,15 +344,39 @@
             total += from_z[j, k].astype(f32)
         out_ref[:, j * width:(j + 1) * width] = total.astype(jnp.bfloat16)
 
-    steps = (after_core, after_one, after_two, finish)
-    for step in range(parts + 4):
-        if step < parts:
-            produce(step)
-        for stage in range(4):
-            j = step - 1 - stage
-            if 0 <= j < parts:
-                arrive(scatters[j][stage])
-                steps[stage](j)
+    produce(0)
+    produce(1)
+    for step in range(count + 3):
+        if step < count:
+            p, b = units[step]
+            if b == 0:
+                arrive(core_copies[2 * p:2 * p + 2])
+            for h in range(2):
+                after_core(2 * p + h, back_order[b])
+                begin(scatters[step][h][0:1])
+            if b == 1 and 2 * p + 2 < parts:
+                produce(2 * p + 2)
+                produce(2 * p + 3)
+        i = step - 1
+        if 0 <= i < count:
+            p, b = units[i]
+            for h in range(2):
+                arrive(scatters[i][h][0:1])
+                after_one(2 * p + h, back_order[b])
+                begin(scatters[i][h][1:2])
+        i = step - 2
+        if 0 <= i < count:
+            p, b = units[i]
+            for h in range(2):
+                arrive(scatters[i][h][1:2])
+                if b < 3:
+                    to_z[2 * p + h, b] = at_z(2 * p + h, back_order[b]).astype(jnp.bfloat16)
+                    begin(scatters[i][h][2:3])
+        i = step - 3
+        if 0 <= i < count and units[i][1] == 3:
+            for h in range(2):
+                arrive([scatters[i - 3 + k][h][2] for k in range(3)])
+                finish(2 * units[i][0] + h)
 
     for copy in started:
         copy.wait_send()
@@ -348,15 +390,11 @@
     quota = max(1, cap // (4 * device_count))
     slots = cap + device_count * quota
     width = model // parts
-    route_weights = scores / jnp.sum(scores, axis=1, keepdims=True)
-    meta = jnp.concatenate(
-        [expert_ids.astype(jnp.float32), backup_ids.astype(jnp.float32), route_weights,
-         jnp.zeros((tok_rows, 128 - 3 * top), jnp.float32)], axis=1)
     bf16, f32 = jnp.bfloat16, jnp.float32
     grid = (4, 2, 2)
     vmem = lambda shape, kind: pltpu.VMEM(shape, kind)
     scratch = [
-        vmem(grid + (2, tok_rows, 128), f32),
+        vmem((128, 128), f32), vmem(grid + (2, tok_rows, 128), f32),
         vmem((parts,) + grid + (2, tok_rows, width), bf16),
         vmem((model, ff), bf16), vmem((model, ff), bf16), vmem((parts, ff, width), bf16),
         vmem((slots, 512), bf16),
@@ -367,8 +405,9 @@
         vmem((parts, 4, 2, tok_rows, width), bf16), vmem((parts, 4, 2, tok_rows, width), bf16),
         vmem((parts, 4, tok_rows, width), bf16), vmem((parts, 4, tok_rows, width), bf16),
         vmem((parts, 3, tok_rows, width), bf16), vmem((parts, 3, tok_rows, width), bf16),
-        pltpu.SemaphoreType.DMA((parts + 1, 6)), pltpu.SemaphoreType.DMA((parts + 1, 6)),
-        pltpu.SemaphoreType.DMA((parts, 6)), pltpu.SemaphoreType.DMA((parts, 6)),
+        pltpu.SemaphoreType.DMA((6,)), pltpu.SemaphoreType.DMA((6,)),
+        pltpu.SemaphoreType.DMA((parts, 15)), pltpu.SemaphoreType.DMA((parts, 15)),
+        pltpu.SemaphoreType.DMA((parts, 13)), pltpu.SemaphoreType.DMA((parts, 13)),
         pltpu.SemaphoreType.DMA((3, parts)),
     ]
     whole = pl.BlockSpec(memory_space=pltpu.VMEM)
@@ -376,17 +415,17 @@
     return pl.pallas_call(
         functools.partial(exchange, (parts, width, cap, quota, slots, top)),
         out_shape=jax.ShapeDtypeStruct((tok_rows, model), bf16),
-        in_specs=[whole, whole, away, away, away],
+        in_specs=[whole, whole, whole, whole, away, away, away],
         out_specs=whole,
         scratch_shapes=scratch,
         compiler_params=pltpu.CompilerParams(
             collective_id=0, has_side_effects=True, vmem_limit_bytes=60 * 1024 * 1024),
-    )(tokens, meta, gate_weight, up_weight, down_weight)
+    )(tokens, expert_ids.T, backup_ids.T, scores.T, gate_weight, up_weight, down_weight)
 
 
 def pick_body(mesh):
     if mesh.shape["gx"] == 4 and mesh.shape["gy"] == 8:
-        return functools.partial(fused_body, 4)
+        return functools.partial(fused_body, 2)
     return on_device
 
 

time: 71.5 us -> 61.6 us (0.86)
  Pallas kernels: 65.8 us -> 59.9 us
  other arithmetic: 2.84 us -> 0 us
  local copies, waits for them, and re-layouts: 2.54 us -> 1.55 us
    pallas_call x1, Pallas kernels: 65.8 us -> 59.9 us  [fused_body(): pl.pallas_call(functools.partial(exchange, (parts, width, cap, quota, slo...]
    convert_element_type x2 -> x0, other arithmetic: 1.38 us -> none  [the longest x1 0.69 us: fused_body(): expert_ids.astype(jnp.float32)]
    unnamed x2 -> x1, local copies, waits for them, and re-layouts: 2.31 us -> 1.55 us
where the time goes in v2:
time: 61.6 us; the launch traced here: 61.4 us
  Pallas kernels  59.9 us (97%)
  local copies, waits for them, and re-layouts  1.55 us (3%)
    pallas_call x1, Pallas kernels, fused_body(): pl.pallas_call(functools.partial(exchange, (parts, width, cap, quota, slo...  59.9 us
    unnamed x1, local copies, waits for them, and re-layouts  1.55 us

profile of v2, /device:TPU:0, one launch (start us, length us, event | category | flops | bytes accessed | tf_op | source)
XLA Modules:
  0.0 61.4 jit_solution(13428029508972210167)
XLA Ops:
  0.0 59.9 %shard_map.73 = bf16[16,3584]{1,0:T(8,128)(2,1)} custom-call(bf16[16,3584]{1,0:T(8,128)(2,1)} %tok_ref.1, s32[8,16]{1,0:T(8,128)} %bitcast.3, s32[8,16]{1,0:T(8,128)} %bitcast.4, f32[8,16]{1,0:T(8,128)} %bitcast.5, bf16[1,3584,1024]{2,1,0:T(8,128)(2,1)} %gate_hbm.1, bf16[1,3584,1024]{2,1,0:T(8,128)(2,1)} %up_hbm.1, bf16[1,1024,3584]{2,1,0:T(8,128)(2,1)} %down_hbm.1), custom_call_target="tpu_custom_call" | custom-call | tf_op jit(solution)/shard_map/pallas_call | solution.py:415
  59.9 1.6 %copy.9 = bf16[16,3584]{1,0:T(8,128)(2,1)} copy(bf16[16,3584]{1,0:T(8,128)(2,1)} %shard_map.73) | data formatting | bytes 229376

commit v3 on v2

--- a/solution.py
+++ b/solution.py
@@ -147,12 +147,9 @@
         pair = [pltpu.make_async_copy(gate_hbm.at[0, rows], wg.at[rows], w_sem.at[0, j]),
                 pltpu.make_async_copy(up_hbm.at[0, rows], wu.at[rows], w_sem.at[1, j])]
         weight_copies.append(pair)
-        for copy in pair:
-            copy.start()
     down_copies = []
     for j in range(parts):
         copy = pltpu.make_async_copy(down_hbm.at[0, :, pl.ds(j * width, width)], wd.at[j], w_sem.at[2, j])
-        copy.start()
         down_copies.append(copy)
 
     barrier = pltpu.get_barrier_semaphore()
@@ -260,6 +257,8 @@
     for p in range(parts // 2):
         for k in range(3):
             begin([token_z[2 * p][k], token_z[2 * p + 1][k]])
+    for copy in [copy for pair in weight_copies for copy in pair] + down_copies:
+        copy.start()
     count = len(units)
     for step in range(count + 3):
         if step == 1:
@@ -268,16 +267,17 @@
         if 2 <= step <= 3:
             arrive(meta_rest[step - 2:step - 1])
             begin(meta_rest[step - 1:step])
+        if 0 < step <= count:
+            arrive(gathers[step - 1][0])
+            begin(gathers[step - 1][1])
         if 0 < step < count:
             p, b = units[step]
             if b > 0:
                 arrive([token_z[2 * p][b - 1], token_z[2 * p + 1][b - 1]])
             begin(gathers[step][0])
-        for stage in (1, 2):
-            i = step - stage
-            if 0 <= i < count:
-                arrive(gathers[i][stage - 1])
-                begin(gathers[i][stage])
+        if 0 <= step - 2 < count:
+            arrive(gathers[step - 2][1])
+            begin(gathers[step - 2][2])
         if step == 4:
             arrive(meta_rest[2:3])
             route()

time: 61.6 us -> 63.9 us (1.037)
  Pallas kernels: 59.9 us -> 62.2 us
    pallas_call x1, Pallas kernels: 59.9 us -> 62.2 us  [fused_body(): pl.pallas_call(functools.partial(exchange, (parts, width, cap, quota, slo...]
where the time goes in v3:
time: 63.9 us; the launch traced here: 63.7 us
  Pallas kernels  62.2 us (97%)
  local copies, waits for them, and re-layouts  1.55 us (2%)
    pallas_call x1, Pallas kernels, fused_body(): pl.pallas_call(functools.partial(exchange, (parts, width, cap, quota, slo...  62.2 us
    unnamed x1, local copies, waits for them, and re-layouts  1.55 us

profile of v3, /device:TPU:0, one launch (start us, length us, event | category | flops | bytes accessed | tf_op | source)
XLA Modules:
  0.0 63.7 jit_solution(1462357263137614581)
XLA Ops:
  0.0 62.2 %shard_map.73 = bf16[16,3584]{1,0:T(8,128)(2,1)} custom-call(bf16[16,3584]{1,0:T(8,128)(2,1)} %tok_ref.1, s32[8,16]{1,0:T(8,128)} %bitcast.3, s32[8,16]{1,0:T(8,128)} %bitcast.4, f32[8,16]{1,0:T(8,128)} %bitcast.5, bf16[1,3584,1024]{2,1,0:T(8,128)(2,1)} %gate_hbm.1, bf16[1,3584,1024]{2,1,0:T(8,128)(2,1)} %up_hbm.1, bf16[1,1024,3584]{2,1,0:T(8,128)(2,1)} %down_hbm.1), custom_call_target="tpu_custom_call" | custom-call | tf_op jit(solution)/shard_map/pallas_call | solution.py:415
  62.2 1.6 %copy.9 = bf16[16,3584]{1,0:T(8,128)(2,1)} copy(bf16[16,3584]{1,0:T(8,128)(2,1)} %shard_map.73) | data formatting | bytes 229376
